TPU v7x, 32 devices: a whole 2x2x4 slice. The times are simulated.
32 devices in a mesh: sector: 8 (over y, x, core), term: 4 (over z).
Axes of the slice: x: 2, y: 2, z: 4, core: 2. Of those that a mesh axis runs over, the one named last changes fastest.
Arguments:
- x_start: float32 [8, 384, 384], P('sector', 'term'), may hold values from -6 to 6
- x_prev: float32 [8, 384, 384], P('sector', 'term'), may hold values from -6 to 6
- precond: float32 [8, 384, 384], P('sector', 'term'), may hold values from 0.5 to 6
- left_env: bfloat16 [256, 384, 384], P(('sector', 'term')), may hold values from -0.20412415 to 1.2041241
- right_env: bfloat16 [256, 384, 384], P(('sector', 'term')), may hold values from -0.20412415 to 1.2041241
- triples: int32 [640, 4], P(('sector', 'term')), may hold values from 0 to 63, as said below
- trip_count: int32 [8, 4], P('sector', 'term'), may hold values from 5 to 20, as said below
- term_coef: float32 [64], replicated, may hold values from 0.25 to 1
- lanczos_beta: float32 [3], replicated, may hold values from 0.3 to 1.2
- block_owner: int32 [8], replicated, may hold values from 0 to 7, each once
Outputs:
- final_vector: float32 [8, 384, 384], P('sector', 'term')
- rayleigh: float32 [3], replicated
Inputs may be any that keep to these rules, and one draw needn't show every extreme that they name: `triples`: Columns: a left slot below 8, a wavefunction block id below 8, a right slot below 8, an operator term below 64. `trip_count`: some device has exactly 20 live triples in every draw. `block_owner`: each sector index holds exactly one block.
All inputs are finite; a program needn't handle non-finite values.
Results may differ from a plain program's by a relative error of at most 0.006.
Values may be sent and summed in bfloat16 or wider, within the bound.
No kernel may reach another device: no remote copies, remote signals or barrier semaphores. Data moves between devices by JAX's collectives and lax.ppermute only.
A program may use at most 64 MiB of HBM per device.

v0:
```python
import math
import jax
import jax.numpy as jnp
from jax import lax
from jax.sharding import PartitionSpec as P

APPS = 3
EPSILON = 1e-06


def local(
    x_start,
    x_prev,
    precond,
    left_env,
    right_env,
    triples,
    trip_count,
    term_coef,
    lanczos_beta,
    block_owner,
):
    sectors = lax.axis_size("sector")
    term_count = lax.axis_size("term")
    block_size = left_env.shape[1]
    share_rows = x_start.shape[1]
    cell_count = sectors * block_size * block_size
    normaliser = 1.0 / math.sqrt(term_count * triples.shape[0])
    live_count = trip_count[0, 0]
    term_match = triples[:, 3:4] == jnp.arange(term_coef.shape[0], dtype=jnp.int32)[None, :]
    coefficient = jnp.sum(jnp.where(term_match, term_coef[None, :], 0.0), axis=1)
    owner_match = triples[:, 1:2] == jnp.arange(sectors, dtype=jnp.int32)[None, :]
    owner_rows = jnp.sum(jnp.where(owner_match, block_owner[None, :], 0), axis=1)

    def own_rows(array):
        return lax.dynamic_slice_in_dim(array, lax.axis_index("term") * share_rows, share_rows, 1)

    current, previous, diagonal = (
        lax.all_gather(x_start, "term", axis=1, tiled=True),
        lax.all_gather(x_prev, "term", axis=1, tiled=True),
        lax.all_gather(precond, "term", axis=1, tiled=True),
    )
    quotients = []
    for position in range(APPS):
        wave_half = current.astype(jnp.bfloat16)
        gathered = lax.all_gather(wave_half, "sector", axis=0, tiled=True)

        def add_triple(triple, accumulated):
            left_block = lax.dynamic_index_in_dim(left_env, triples[triple, 0], 0, keepdims=False)
            wave_block = lax.dynamic_index_in_dim(gathered, owner_rows[triple], 0, keepdims=False)
            right_block = lax.dynamic_index_in_dim(right_env, triples[triple, 2], 0, keepdims=False)
            middle = jnp.dot(left_block, wave_block, preferred_element_type=jnp.float32).astype(
                jnp.bfloat16
            )
            product = jnp.dot(middle, right_block, preferred_element_type=jnp.float32)
            return accumulated + coefficient[triple] * product

        start_sum = jnp.zeros((block_size, block_size), jnp.float32)
        applied = (lax.fori_loop(0, live_count, add_triple, start_sum) * normaliser)[None]
        applied = lax.psum(applied, "term")
        beta_now = lanczos_beta[position]
        cur_own = own_rows(current)
        app_own = own_rows(applied)
        prev_own = own_rows(previous)
        diag_own = own_rows(diagonal)
        diag_square = diag_own * diag_own
        weighted = diag_square * app_own
        weighted_cur = diag_square * cur_own
        sums_all = lax.psum(
            (
                jnp.sum(cur_own * app_own),
                jnp.sum(cur_own * cur_own),
                jnp.sum(weighted * app_own),
                jnp.sum(weighted * cur_own),
                jnp.sum(weighted * prev_own),
                jnp.sum(weighted_cur * cur_own),
                jnp.sum(weighted_cur * prev_own),
                jnp.sum(diag_square * prev_own * prev_own),
            ),
            ("sector", "term"),
        )
        (
            cross_sum,
            self_sum,
            image_image,
            image_current,
            image_previous,
            current_current,
            current_previous,
            previous_previous,
        ) = sums_all
        quotient = cross_sum / self_sum
        square_sum = (
            image_image
            - 2.0 * quotient * image_current
            - 2.0 * beta_now * image_previous
            + quotient * quotient * current_current
            + 2.0 * quotient * beta_now * current_previous
            + beta_now * beta_now * previous_previous
        )
        residual = applied - quotient * current - beta_now * previous
        scaled = diagonal * residual
        following = scaled / jnp.sqrt(square_sum / cell_count + EPSILON)
        previous, current = (current, following)
        quotients.append(quotient)
    return (own_rows(current), jnp.stack(quotients))


def solution(mesh):
    placed = (
        P("sector", "term", None),
        P("sector", "term", None),
        P("sector", "term", None),
        P(("sector", "term"), None, None),
        P(("sector", "term"), None, None),
        P(("sector", "term"), None),
        P("sector", "term"),
        P(),
        P(),
        P(),
    )
    return jax.shard_map(
        local,
        mesh=mesh,
        in_specs=placed,
        out_specs=(P("sector", "term", None), P()),
        check_vma=False,
    )
```

profile of v0, /device:TPU:0, one launch (start us, length us, event | category | flops | bytes accessed | tf_op | source)
XLA Modules:
  0.0 1039.4 jit_solution(10864611968168883217)
XLA Ops:
  7.2 18.5 %all_gather.19 = f32[1,384,384]{2,1,0:T(8,128)S(1)} all-gather(f32[1,96,384]{2,1,0:T(8,128)} %param.16), channel_id=1, replica_groups=mesh['sector'=8,'term'=4] {'term'}, dimensions={1}, use_global_device_ids=true | all-gather | bytes 737280 | tf_op jit(solution)/shard_map/all_gather | solution.py:39
  25.7 0.8 convert_element_type.18
  26.5 0.8 slice_bitcast_fusion
  27.3 0.8 select_reduce_fusion
  28.1 0.7 select_reduce_fusion.1
  28.9 27.8 %all-gather.4.cloned.1.call-done = bf16[8,384,384]{2,1,0:T(8,128)(2,1)} async-done(((bf16[1,384,384]{2,1,0:T(8,128)(2,1)}), bf16[8,384,384]{2,1,0:T(8,128)(2,1)}) %all-gather.4.cloned.1.call-update) | async-done | bytes 2359312 | tf_op jit(solution)/shard_map/all_gather | solution.py:46
  56.8 105.1 %while.30 = (s32[]{:T(128)}, f32[384,384]{1,0:T(8,128)S(1)}, s32[]{:T(128)}, f32[20]{0:T(128)S(1)}, s32[20,4]{0,1:T(4,128)S(1)}, /*index=5*/bf16[8,384,384]{2,1,...) while((s32[]{:T(128)}, f32[384,384]{1,0:T(8,128)S(1)}, ...), condition=%wide.region_3.4_spmd, body=%wide.region_2.3_spmd.sunk | while | flops 226934800 | bytes 2065213 | solution.py:59
  64.8 2.4 fusion.58
  75.3 2.4 fusion.58
  85.7 2.4 fusion.58
  96.1 2.4 fusion.58
  106.6 2.4 fusion.58
  117.0 2.4 fusion.58
  127.5 2.4 fusion.58
  137.9 2.4 fusion.58
  148.4 2.4 fusion.58
  158.8 2.4 fusion.58
  161.9 0.9 multiply_bitcast_fusion.2
  165.4 33.6 %all_gather.18 = f32[1,384,384]{2,1,0:T(8,128)S(1)} all-gather(f32[1,96,384]{2,1,0:T(8,128)S(1)} %copy-done), channel_id=1, replica_groups=mesh['sector'=8,'term'=4] {'term'}, dimensions={1}, use_global_device_ids=true | all-gather | bytes 737280 | tf_op jit(solution)/shard_map/all_gather | solution.py:41
  199.0 16.4 %all_gather.21 = f32[1,384,384]{2,1,0:T(8,128)S(1)} all-gather(f32[1,96,384]{2,1,0:T(8,128)S(1)} %copy-done.1), channel_id=1, replica_groups=mesh['sector'=8,'term'=4] {'term'}, dimensions={1}, use_global_device_ids=true | all-gather | bytes 737280 | tf_op jit(solution)/shard_map/all_gather | solution.py:40
  215.4 97.2 %all-reduce.7.cloned.1.call-done = f32[1,384,384]{2,1,0:T(8,128)} async-done(((f32[1,384,384]{2,1,0:T(8,128)}), f32[1,384,384]{2,1,0:T(8,128)}) %all-reduce.7.cloned.1.call-update) | async-done | bytes 589840 | tf_op jit(solution)/shard_map/psum | solution.py:60
  312.6 1.7 fusion.39
  314.3 42.7 %all-reduce.2 = (f32[]{:T(128)}, f32[]{:T(128)}, f32[]{:T(128)}, f32[]{:T(128)}, f32[]{:T(128)}, /*index=5*/f32[]{:T(128)}, f32[]{:T(128)}, f32[]{:T(128)}) all-reduce(f32[]{:T(128)} %get-tuple-element.167, f32[]{:T(128)} %get-tuple-element.166, f32[]{:T(128)} %get-tuple-element.168, ...), channel_id=1, replica_groups=mesh['sector'=8,'term'=4] {'sector','term'}, use_global_device_ids=true, to_apply=%region_10.11 | all-reduce | flops 8 | bytes 64 | tf_op jit(solution)/shard_map/psum | solution.py:69
  362.8 2.5 fusion.41
  365.4 29.6 %all-gather.6.cloned.1.call-done = bf16[8,384,384]{2,1,0:T(8,128)(2,1)} async-done(((bf16[1,384,384]{2,1,0:T(8,128)(2,1)}), bf16[8,384,384]{2,1,0:T(8,128)(2,1)}) %all-gather.6.cloned.1.call-update) | async-done | bytes 2359312 | tf_op jit(solution)/shard_map/all_gather | solution.py:46
  395.1 105.1 %while.31 = (s32[]{:T(128)}, f32[384,384]{1,0:T(8,128)S(1)}, s32[]{:T(128)}, f32[20]{0:T(128)S(1)}, s32[20,4]{0,1:T(4,128)S(1)}, /*index=5*/bf16[8,384,384]{2,1,...) while((s32[]{:T(128)}, f32[384,384]{1,0:T(8,128)S(1)}, ...), condition=%wide.region_22.23_spmd, body=%wide.region_21.22_spmd.sunk | while | flops 226934800 | bytes 2065213 | solution.py:59
  403.1 2.4 fusion.62
  413.5 2.4 fusion.62
  423.9 2.4 fusion.62
  434.4 2.4 fusion.62
  444.8 2.4 fusion.62
  455.3 2.4 fusion.62
  465.7 2.4 fusion.62
  476.2 2.4 fusion.62
  486.6 2.4 fusion.62
  497.0 2.4 fusion.62
  500.1 0.9 multiply_bitcast_fusion.1
  503.8 140.3 %all-reduce.9.cloned.1.call-done = f32[1,384,384]{2,1,0:T(8,128)} async-done(((f32[1,384,384]{2,1,0:T(8,128)}), f32[1,384,384]{2,1,0:T(8,128)}) %all-reduce.9.cloned.1.call-update) | async-done | bytes 589840 | tf_op jit(solution)/shard_map/psum | solution.py:60
  644.1 1.7 multiply_reduce_fusion.7
  645.8 40.3 %all-reduce.1 = (f32[]{:T(128)}, f32[]{:T(128)}, f32[]{:T(128)}, f32[]{:T(128)}, f32[]{:T(128)}, /*index=5*/f32[]{:T(128)}, f32[]{:T(128)}) all-reduce(f32[]{:T(128)} %get-tuple-element.159, f32[]{:T(128)} %get-tuple-element.160, f32[]{:T(128)} %get-tuple-element.170, ...), channel_id=1, replica_groups=mesh['sector'=8,'term'=4] {'sector','term'}, use_global_device_ids=true, to_apply=%region_29.30 | all-reduce | flops 7 | bytes 56 | tf_op jit(solution)/shard_map/psum | solution.py:69
  691.3 2.6 fusion.40
  694.0 28.5 %all-gather.8.cloned.1.call-done = bf16[8,384,384]{2,1,0:T(8,128)(2,1)} async-done(((bf16[1,384,384]{2,1,0:T(8,128)(2,1)}), bf16[8,384,384]{2,1,0:T(8,128)(2,1)}) %all-gather.8.cloned.1.call-update) | async-done | bytes 2359312 | tf_op jit(solution)/shard_map/all_gather | solution.py:46
  722.5 110.6 %while.32 = (s32[]{:T(128)}, f32[384,384]{1,0:T(8,128)S(1)}, s32[]{:T(128)}, f32[20]{0:T(128)S(1)}, s32[20,4]{0,1:T(4,128)S(1)}, /*index=5*/bf16[8,384,384]{2,1,...) while((s32[]{:T(128)}, f32[384,384]{1,0:T(8,128)S(1)}, ...), condition=%wide.region_39.40_spmd, body=%wide.region_38.39_spmd.sunk | while | flops 226934800 | bytes 2065213 | solution.py:59
  727.6 0.7 dynamic_slice.282
  731.0 2.5 fusion.66
  738.6 0.7 dynamic_slice.282
  742.0 2.5 fusion.66
  752.3 0.7 dynamic_slice.283
  753.0 2.5 fusion.66
  764.0 2.5 fusion.66
  771.6 0.7 dynamic_slice.282
  775.0 2.5 fusion.66
  782.6 0.7 dynamic_slice.282
  786.0 2.5 fusion.66
  796.3 0.7 dynamic_slice.283
  797.0 2.5 fusion.66
  808.0 2.5 fusion.66
  819.0 2.5 fusion.66
  830.0 2.5 fusion.66
  833.1 0.9 multiply_bitcast_fusion
  836.4 146.3 %all-reduce.11.cloned.1.call-done = f32[1,384,384]{2,1,0:T(8,128)} async-done(((f32[1,384,384]{2,1,0:T(8,128)}), f32[1,384,384]{2,1,0:T(8,128)}) %all-reduce.11.cloned.1.call-update) | async-done | bytes 589840 | tf_op jit(solution)/shard_map/psum | solution.py:60
  982.7 1.7 multiply_reduce_fusion
  984.3 40.3 %all-reduce = (f32[]{:T(128)}, f32[]{:T(128)}, f32[]{:T(128)}, f32[]{:T(128)}, f32[]{:T(128)}, /*index=5*/f32[]{:T(128)}, f32[]{:T(128)}) all-reduce(f32[]{:T(128)} %get-tuple-element.152, f32[]{:T(128)} %get-tuple-element.153, f32[]{:T(128)} %get-tuple-element.169, ...), channel_id=1, replica_groups=mesh['sector'=8,'term'=4] {'sector','term'}, use_global_device_ids=true, to_apply=%region_46.47 | all-reduce | flops 7 | bytes 56 | tf_op jit(solution)/shard_map/psum | solution.py:69
  1030.3 2.2 multiply_divide_fusion.2
  (109 shorter events, 53.0 us)
Async XLA Ops:
  7.2 49.6 %copy-start.2 = (s32[20,4]{0,1:T(4,128)S(1)}, s32[20,4]{0,1:T(4,128)}, u32[]{:S(2)}) copy-start(s32[20,4]{0,1:T(4,128)} %param.21) | copy-start | bytes 964
  7.2 49.5 %all-gather.4.cloned.1.call-start = ((), (), s32[]{:S(2)}) async-start(), calls=%async_computation | async-start | bytes 2654208 | tf_op jit(solution)/shard_map/all_gather | solution.py:46
  26.5 286.1 %all-reduce.7.cloned.1.call-start = ((), (), s32[]{:S(2)}) async-start(), calls=%async_computation.1 | async-start | bytes 1179648 | tf_op jit(solution)/shard_map/psum | solution.py:60
  56.8 106.1 %copy-start.3 = (f32[3]{0:T(128)S(1)}, f32[3]{0:T(128)}, u32[]{:S(2)}) copy-start(f32[3]{0:T(128)} %param.24) | copy-start | bytes 40
  56.8 108.6 %copy-start = (f32[1,96,384]{2,1,0:T(8,128)S(1)}, f32[1,96,384]{2,1,0:T(8,128)}, u32[]{:S(2)}) copy-start(f32[1,96,384]{2,1,0:T(8,128)} %param.18) | copy-start | bytes 442372
  161.9 37.1 %copy-start.1 = (f32[1,96,384]{2,1,0:T(8,128)S(1)}, f32[1,96,384]{2,1,0:T(8,128)}, u32[]{:S(2)}) copy-start(f32[1,96,384]{2,1,0:T(8,128)} %param.17) | copy-start | bytes 442372
  162.8 232.2 %all-gather.6.cloned.1.call-start = ((), (), s32[]{:S(2)}) async-start(), calls=%async_computation.2 | async-start | bytes 2654208 | tf_op jit(solution)/shard_map/all_gather | solution.py:46
  365.3 278.8 %all-reduce.9.cloned.1.call-start = ((), (), s32[]{:S(2)}) async-start(), calls=%async_computation.3 | async-start | bytes 1179648 | tf_op jit(solution)/shard_map/psum | solution.py:60
  501.0 221.4 %all-gather.8.cloned.1.call-start = ((), (), s32[]{:S(2)}) async-start(), calls=%async_computation.4 | async-start | bytes 2654208 | tf_op jit(solution)/shard_map/all_gather | solution.py:46
  693.9 288.7 %all-reduce.11.cloned.1.call-start = ((), (), s32[]{:S(2)}) async-start(), calls=%async_computation.5 | async-start | bytes 1179648 | tf_op jit(solution)/shard_map/psum | solution.py:60
Sparse Core Ops, SparseCore 0:
  26.6 30.0 all-gather.3
  162.9 149.6 all-reduce.6
  365.5 29.5 all-gather.5
  501.1 142.9 all-reduce.8
  694.0 28.3 all-gather.7
  834.1 148.4 all-reduce.10
where the time goes:
time: 1050 us; the launch traced here: 1040 us
  waiting for transfers between devices  470 us (45%)
  blocking collectives  192 us (18%)
  loops' own time  192 us (18%)
  matrix products  73.7 us (7%)
  local copies, waits for them, and re-layouts  56.9 us (5%)
  between operations  37.2 us (4%)
  other arithmetic  17.8 us (2%)
    psum x3, waiting for transfers between devices, local(): applied = lax.psum(applied, 'term')  384 us
    another operation x3, loops' own time, local(): lax.fori_loop(0, live_count, add_triple, start_sum) * normaliser  192 us
    psum x3, blocking collectives, local(): lax.psum((jnp.sum(cur_own * app_own), jnp.sum(cur_own * cur_own), jnp.sum...  123 us
    all_gather x3, waiting for transfers between devices, local(): gathered = lax.all_gather(wave_half, 'sector', axis=0, tiled=True)  86 us
    dot_general x30, matrix products, add_triple(): product = jnp.dot(middle, right_block, preferred_element_type=jnp.float32)  73.7 us
    all_gather x1, blocking collectives, local(): lax.all_gather(precond, 'term', axis=1, tiled=True)  33.6 us
  transfers between devices with their start and end apart: 6, of which 6 were waited for; matrix products, arithmetic and copies ran while one was open for 0% of the time, Pallas kernels for 0%

commit v1 on v0

--- a/solution.py
+++ b/solution.py
@@ -57,7 +57,19 @@
 
         start_sum = jnp.zeros((block_size, block_size), jnp.float32)
         applied = (lax.fori_loop(0, live_count, add_triple, start_sum) * normaliser)[None]
-        applied = lax.psum(applied, "term")
+
+        def order_streams(unit):
+            k_all = lax.axis_size("term")
+            arr_next = unit
+            for d in [jj for jj in (1, 2, 4, 8, 16) if jj < k_all]:
+                panels = []
+                for i in tuple(range(k_all)):
+                    panels.append((i, i ^ d))
+                t_next = lax.ppermute(arr_next, axis_name="term", perm=panels)
+                arr_next = arr_next + t_next
+            return arr_next
+
+        applied = order_streams(applied)
         beta_now = lanczos_beta[position]
         cur_own = own_rows(current)
         app_own = own_rows(applied)

time: 1050 us -> 1050 us (level)
  waiting for transfers between devices: 470 us -> 142 us
  blocking collectives: 192 us -> 459 us
  starting transfers between devices: 0.25 us -> 68.7 us
    psum x3 -> x0, waiting for transfers between devices: 384 us -> none  [local(): applied = lax.psum(applied, 'term')]
    psum x3, blocking collectives: 123 us -> 403 us  [local(): lax.psum((jnp.sum(cur_own * app_own), jnp.sum(cur_own * cur_own), jnp.sum...]
    ppermute x0 -> x6, starting transfers between devices: none -> 68.6 us  [order_streams(): t_next = lax.ppermute(arr_next, axis_name='term', perm=panels)]
    ppermute x0 -> x6, waiting for transfers between devices: none -> 52.7 us  [order_streams(): t_next = lax.ppermute(arr_next, axis_name='term', perm=panels)]
    all_gather x1, blocking collectives: 33.6 us -> 22.5 us  [local(): lax.all_gather(precond, 'term', axis=1, tiled=True)]
  transfers between devices with their start and end apart: 6 -> 9, of which waited for: 6 -> 8; matrix products, arithmetic and copies ran while one was open for 0% -> 0% of each run, Pallas kernels for 0% -> 0%
where the time goes in v1:
time: 1050 us; the launch traced here: 1040 us
  blocking collectives  459 us (44%)
  loops' own time  192 us (18%)
  waiting for transfers between devices  142 us (14%)
  matrix products  73.7 us (7%)
  starting transfers between devices  68.7 us (7%)
  local copies, waits for them, and re-layouts  56.9 us (5%)
  between operations  37.3 us (4%)
    psum x3, blocking collectives, local(): lax.psum((jnp.sum(cur_own * app_own), jnp.sum(cur_own * cur_own), jnp.sum...  403 us
    another operation x3, loops' own time, local(): lax.fori_loop(0, live_count, add_triple, start_sum) * normaliser  192 us
    all_gather x3, waiting for transfers between devices, local(): gathered = lax.all_gather(wave_half, 'sector', axis=0, tiled=True)  89.1 us
    dot_general x30, matrix products, add_triple(): product = jnp.dot(middle, right_block, preferred_element_type=jnp.float32)  73.7 us
    ppermute x6, starting transfers between devices, order_streams(): t_next = lax.ppermute(arr_next, axis_name='term', perm=panels)  68.6 us
    ppermute x6, waiting for transfers between devices, order_streams(): t_next = lax.ppermute(arr_next, axis_name='term', perm=panels)  52.7 us
    all_gather x1, blocking collectives, local(): lax.all_gather(precond, 'term', axis=1, tiled=True)  22.5 us
  transfers between devices with their start and end apart: 9, of which 8 were waited for; matrix products, arithmetic and copies ran while one was open for 0% of the time, Pallas kernels for 0%

profile of v1, /device:TPU:0, one launch (start us, length us, event | category | flops | bytes accessed | tf_op | source)
XLA Modules:
  0.0 1039.7 jit_solution(1599666440263608965)
XLA Ops:
  7.2 18.5 %all_gather.19 = f32[1,384,384]{2,1,0:T(8,128)S(1)} all-gather(f32[1,96,384]{2,1,0:T(8,128)} %param.16), channel_id=1, replica_groups=mesh['sector'=8,'term'=4] {'term'}, dimensions={1}, use_global_device_ids=true | all-gather | bytes 737280 | tf_op jit(solution)/shard_map/all_gather | solution.py:39
  25.7 0.8 convert_element_type.18
  26.5 0.8 slice_bitcast_fusion
  27.3 0.8 select_reduce_fusion
  28.1 0.7 select_reduce_fusion.1
  28.9 27.8 %all-gather.4.cloned.1.call-done = bf16[8,384,384]{2,1,0:T(8,128)(2,1)} async-done(((bf16[1,384,384]{2,1,0:T(8,128)(2,1)}), bf16[8,384,384]{2,1,0:T(8,128)(2,1)}) %all-gather.4.cloned.1.call-update) | async-done | bytes 2359312 | tf_op jit(solution)/shard_map/all_gather | solution.py:46
  56.8 105.1 %while.30 = (s32[]{:T(128)}, f32[384,384]{1,0:T(8,128)S(1)}, s32[]{:T(128)}, f32[20]{0:T(128)S(1)}, s32[20,4]{0,1:T(4,128)S(1)}, /*index=5*/bf16[8,384,384]{2,1,...) while((s32[]{:T(128)}, f32[384,384]{1,0:T(8,128)S(1)}, ...), condition=%wide.region_3.4_spmd, body=%wide.region_2.3_spmd.sunk | while | flops 226934800 | bytes 2065213 | solution.py:59
  64.8 2.4 fusion.61
  75.2 2.4 fusion.61
  85.6 2.4 fusion.61
  96.1 2.4 fusion.61
  106.5 2.4 fusion.61
  117.0 2.4 fusion.61
  127.4 2.4 fusion.61
  137.9 2.4 fusion.61
  148.3 2.4 fusion.61
  158.7 2.4 fusion.61
  161.9 22.4 %collective-permute-start = (f32[1,384,384]{2,1,0:T(8,128)S(1)}, f32[1,384,384]{2,1,0:T(8,128)S(1)}, u32[]{:S(2)}, u32[]{:S(2)}) collective-permute-start(f32[1,384,384]{2,1,0:T(8,128)S(1)} %multiply_bitcast_fusion.2), channel_id=1, source_target_pairs={{0,1},{1,0},{2,3},{3,2},{4,5},{5,4},{6,7},{7,6},{8,9},{9,8},{10,11... | collective-permute-start | bytes 1769480 | tf_op jit(solution)/shard_map/ppermute | solution.py:68
  184.4 7.9 collective-permute-done
  195.1 22.5 %all_gather.18 = f32[1,384,384]{2,1,0:T(8,128)S(1)} all-gather(f32[1,96,384]{2,1,0:T(8,128)S(1)} %copy-done), channel_id=1, replica_groups=mesh['sector'=8,'term'=4] {'term'}, dimensions={1}, use_global_device_ids=true | all-gather | bytes 737280 | tf_op jit(solution)/shard_map/all_gather | solution.py:41
  217.6 15.1 %all_gather.21 = f32[1,384,384]{2,1,0:T(8,128)S(1)} all-gather(f32[1,96,384]{2,1,0:T(8,128)S(1)} %copy-done.1), channel_id=1, replica_groups=mesh['sector'=8,'term'=4] {'term'}, dimensions={1}, use_global_device_ids=true | all-gather | bytes 737280 | tf_op jit(solution)/shard_map/all_gather | solution.py:40
  232.8 0.8 fusion.39
  233.6 136.6 %all-reduce.2 = (f32[]{:T(128)}, f32[]{:T(128)}, f32[]{:T(128)}, f32[]{:T(128)}, f32[]{:T(128)}, /*index=5*/f32[]{:T(128)}, f32[]{:T(128)}, f32[]{:T(128)}) all-reduce(f32[]{:T(128)} %get-tuple-element.167, f32[]{:T(128)} %get-tuple-element.166, f32[]{:T(128)} %get-tuple-element.168, ...), channel_id=1, replica_groups=mesh['sector'=8,'term'=4] {'sector','term'}, use_global_device_ids=true, to_apply=%region_9.10 | all-reduce | flops 8 | bytes 64 | tf_op jit(solution)/shard_map/psum | solution.py:81
  376.0 1.5 fusion.44
  377.6 30.3 %all-gather.6.cloned.1.call-done = bf16[8,384,384]{2,1,0:T(8,128)(2,1)} async-done(((bf16[1,384,384]{2,1,0:T(8,128)(2,1)}), bf16[8,384,384]{2,1,0:T(8,128)(2,1)}) %all-gather.6.cloned.1.call-update) | async-done | bytes 2359312 | tf_op jit(solution)/shard_map/all_gather | solution.py:46
  407.9 105.1 %while.31 = (s32[]{:T(128)}, f32[384,384]{1,0:T(8,128)S(1)}, s32[]{:T(128)}, f32[20]{0:T(128)S(1)}, s32[20,4]{0,1:T(4,128)S(1)}, /*index=5*/bf16[8,384,384]{2,1,...) while((s32[]{:T(128)}, f32[384,384]{1,0:T(8,128)S(1)}, ...), condition=%wide.region_21.22_spmd, body=%wide.region_20.21_spmd.sunk | while | flops 226934800 | bytes 2065213 | solution.py:59
  415.9 2.4 fusion.65
  426.3 2.4 fusion.65
  436.8 2.4 fusion.65
  447.2 2.4 fusion.65
  457.7 2.4 fusion.65
  468.1 2.4 fusion.65
  478.6 2.4 fusion.65
  489.0 2.4 fusion.65
  499.4 2.4 fusion.65
  509.9 2.4 fusion.65
  513.0 22.4 %collective-permute-start.2 = (f32[1,384,384]{2,1,0:T(8,128)S(1)}, f32[1,384,384]{2,1,0:T(8,128)S(1)}, u32[]{:S(2)}, u32[]{:S(2)}) collective-permute-start(f32[1,384,384]{2,1,0:T(8,128)S(1)} %multiply_bitcast_fusion.1), channel_id=1, source_target_pairs={{0,1},{1,0},{2,3},{3,2},{4,5},{5,4},{6,7},{7,6},{8,9},{9,8},{10,11... | collective-permute-start | bytes 1769480 | tf_op jit(solution)/shard_map/ppermute | solution.py:68
  535.5 7.9 collective-permute-done.2
  546.3 14.3 %collective-permute-done.3 = f32[1,384,384]{2,1,0:T(8,128)S(1)} collective-permute-done((f32[1,384,384]{2,1,0:T(8,128)S(1)}, f32[1,384,384]{2,1,0:T(8,128)S(1)}, u32[]{:S(2)}, u32[]{:S(2)}) %collective-permute-start.3) | collective-permute-done | bytes 589856 | tf_op jit(solution)/shard_map/ppermute | solution.py:68
  560.6 0.8 multiply_reduce_fusion.7
  561.4 131.1 %all-reduce.1 = (f32[]{:T(128)}, f32[]{:T(128)}, f32[]{:T(128)}, f32[]{:T(128)}, f32[]{:T(128)}, /*index=5*/f32[]{:T(128)}, f32[]{:T(128)}) all-reduce(f32[]{:T(128)} %get-tuple-element.159, f32[]{:T(128)} %get-tuple-element.160, f32[]{:T(128)} %get-tuple-element.170, ...), channel_id=1, replica_groups=mesh['sector'=8,'term'=4] {'sector','term'}, use_global_device_ids=true, to_apply=%region_27.28 | all-reduce | flops 7 | bytes 56 | tf_op jit(solution)/shard_map/psum | solution.py:81
  697.8 1.5 fusion.43
  699.3 31.0 %all-gather.8.cloned.1.call-done = bf16[8,384,384]{2,1,0:T(8,128)(2,1)} async-done(((bf16[1,384,384]{2,1,0:T(8,128)(2,1)}), bf16[8,384,384]{2,1,0:T(8,128)(2,1)}) %all-gather.8.cloned.1.call-update) | async-done | bytes 2359312 | tf_op jit(solution)/shard_map/all_gather | solution.py:46
  730.4 110.6 %while.32 = (s32[]{:T(128)}, f32[384,384]{1,0:T(8,128)S(1)}, s32[]{:T(128)}, f32[20]{0:T(128)S(1)}, s32[20,4]{0,1:T(4,128)S(1)}, /*index=5*/bf16[8,384,384]{2,1,...) while((s32[]{:T(128)}, f32[384,384]{1,0:T(8,128)S(1)}, ...), condition=%wide.region_37.38_spmd, body=%wide.region_36.37_spmd.sunk | while | flops 226934800 | bytes 2065213 | solution.py:59
  738.9 2.5 fusion.69
  749.2 0.7 dynamic_slice.283
  749.9 2.5 fusion.69
  757.5 0.7 dynamic_slice.282
  760.9 2.5 fusion.69
  771.2 0.7 dynamic_slice.283
  771.9 2.5 fusion.69
  782.2 0.7 dynamic_slice.283
  782.9 2.5 fusion.69
  793.9 2.5 fusion.69
  804.9 2.5 fusion.69
  815.9 2.5 fusion.69
  826.9 2.5 fusion.69
  837.9 2.5 fusion.69
  841.1 23.5 %collective-permute-start.4 = (f32[1,384,384]{2,1,0:T(8,128)S(1)}, f32[1,384,384]{2,1,0:T(8,128)S(1)}, u32[]{:S(2)}, u32[]{:S(2)}) collective-permute-start(f32[1,384,384]{2,1,0:T(8,128)S(1)} %multiply_bitcast_fusion), channel_id=1, source_target_pairs={{0,1},{1,0},{2,3},{3,2},{4,5},{5,4},{6,7},{7,6},{8,9},{9,8},{10,11... | collective-permute-start | bytes 1769480 | tf_op jit(solution)/shard_map/ppermute | solution.py:68
  864.6 7.9 collective-permute-done.4
  875.0 14.8 %collective-permute-done.5 = f32[1,384,384]{2,1,0:T(8,128)S(1)} collective-permute-done((f32[1,384,384]{2,1,0:T(8,128)S(1)}, f32[1,384,384]{2,1,0:T(8,128)S(1)}, u32[]{:S(2)}, u32[]{:S(2)}) %collective-permute-start.5) | collective-permute-done | bytes 589856 | tf_op jit(solution)/shard_map/ppermute | solution.py:68
  889.8 0.8 multiply_reduce_fusion
  890.6 135.6 %all-reduce = (f32[]{:T(128)}, f32[]{:T(128)}, f32[]{:T(128)}, f32[]{:T(128)}, f32[]{:T(128)}, /*index=5*/f32[]{:T(128)}, f32[]{:T(128)}) all-reduce(f32[]{:T(128)} %get-tuple-element.152, f32[]{:T(128)} %get-tuple-element.153, f32[]{:T(128)} %get-tuple-element.169, ...), channel_id=1, replica_groups=mesh['sector'=8,'term'=4] {'sector','term'}, use_global_device_ids=true, to_apply=%region_43.44 | all-reduce | flops 7 | bytes 56 | tf_op jit(solution)/shard_map/psum | solution.py:81
  1031.4 1.3 multiply_divide_fusion.2
  (118 shorter events, 55.0 us)
Async XLA Ops:
  7.2 49.6 %copy-start.2 = (s32[20,4]{0,1:T(4,128)S(1)}, s32[20,4]{0,1:T(4,128)}, u32[]{:S(2)}) copy-start(s32[20,4]{0,1:T(4,128)} %param.21) | copy-start | bytes 964
  7.2 49.5 %all-gather.4.cloned.1.call-start = ((), (), s32[]{:S(2)}) async-start(), calls=%async_computation | async-start | bytes 2654208 | tf_op jit(solution)/shard_map/all_gather | solution.py:46
  26.5 381.4 %all-gather.6.cloned.1.call-start = ((), (), s32[]{:S(2)}) async-start(), calls=%async_computation.1 | async-start | bytes 2654208 | tf_op jit(solution)/shard_map/all_gather | solution.py:46
  161.8 30.5 %copy-start.3 = (f32[3]{0:T(128)S(1)}, f32[3]{0:T(128)}, u32[]{:S(2)}) copy-start(f32[3]{0:T(128)} %param.24) | copy-start | bytes 40
  161.9 33.3 %copy-start = (f32[1,96,384]{2,1,0:T(8,128)S(1)}, f32[1,96,384]{2,1,0:T(8,128)}, u32[]{:S(2)}) copy-start(f32[1,96,384]{2,1,0:T(8,128)} %param.18) | copy-start | bytes 442372
  161.9 55.8 %copy-start.1 = (f32[1,96,384]{2,1,0:T(8,128)S(1)}, f32[1,96,384]{2,1,0:T(8,128)}, u32[]{:S(2)}) copy-start(f32[1,96,384]{2,1,0:T(8,128)} %param.17) | copy-start | bytes 442372
  161.9 30.3 %collective-permute-start = (f32[1,384,384]{2,1,0:T(8,128)S(1)}, f32[1,384,384]{2,1,0:T(8,128)S(1)}, u32[]{:S(2)}, u32[]{:S(2)}) collective-permute-start(f32[1,384,384]{2,1,0:T(8,128)S(1)} %multiply_bitcast_fusion.2), channel_id=1, source_target_pairs={{0,1},{1,0},{2,3},{3,2},{4,5},{5,4},{6,7},{7,6},{8,9},{9,8},{10,11... | collective-permute-start | bytes 1769480 | tf_op jit(solution)/shard_map/ppermute | solution.py:68
  192.3 40.4 %collective-permute-start.1 = (f32[1,384,384]{2,1,0:T(8,128)S(1)}, f32[1,384,384]{2,1,0:T(8,128)S(1)}, u32[]{:S(2)}, u32[]{:S(2)}) collective-permute-start(f32[1,384,384]{2,1,0:T(8,128)S(1)} %fusion.40), channel_id=1, source_target_pairs={{0,2},{1,3},{2,0},{3,1},{4,6},{5,7},{6,4},{7,5},{8,10},{9,11},{10,... | collective-permute-start | bytes 1769480 | tf_op jit(solution)/shard_map/ppermute | solution.py:68
  377.6 352.8 %all-gather.8.cloned.1.call-start = ((), (), s32[]{:S(2)}) async-start(), calls=%async_computation.2 | async-start | bytes 2654208 | tf_op jit(solution)/shard_map/all_gather | solution.py:46
  513.0 30.3 %collective-permute-start.2 = (f32[1,384,384]{2,1,0:T(8,128)S(1)}, f32[1,384,384]{2,1,0:T(8,128)S(1)}, u32[]{:S(2)}, u32[]{:S(2)}) collective-permute-start(f32[1,384,384]{2,1,0:T(8,128)S(1)} %multiply_bitcast_fusion.1), channel_id=1, source_target_pairs={{0,1},{1,0},{2,3},{3,2},{4,5},{5,4},{6,7},{7,6},{8,9},{9,8},{10,11... | collective-permute-start | bytes 1769480 | tf_op jit(solution)/shard_map/ppermute | solution.py:68
  543.4 17.2 %collective-permute-start.3 = (f32[1,384,384]{2,1,0:T(8,128)S(1)}, f32[1,384,384]{2,1,0:T(8,128)S(1)}, u32[]{:S(2)}, u32[]{:S(2)}) collective-permute-start(f32[1,384,384]{2,1,0:T(8,128)S(1)} %fusion.41), channel_id=1, source_target_pairs={{0,2},{1,3},{2,0},{3,1},{4,6},{5,7},{6,4},{7,5},{8,10},{9,11},{10,... | collective-permute-start | bytes 1769480 | tf_op jit(solution)/shard_map/ppermute | solution.py:68
  841.1 31.4 %collective-permute-start.4 = (f32[1,384,384]{2,1,0:T(8,128)S(1)}, f32[1,384,384]{2,1,0:T(8,128)S(1)}, u32[]{:S(2)}, u32[]{:S(2)}) collective-permute-start(f32[1,384,384]{2,1,0:T(8,128)S(1)} %multiply_bitcast_fusion), channel_id=1, source_target_pairs={{0,1},{1,0},{2,3},{3,2},{4,5},{5,4},{6,7},{7,6},{8,9},{9,8},{10,11... | collective-permute-start | bytes 1769480 | tf_op jit(solution)/shard_map/ppermute | solution.py:68
  872.6 17.2 %collective-permute-start.5 = (f32[1,384,384]{2,1,0:T(8,128)S(1)}, f32[1,384,384]{2,1,0:T(8,128)S(1)}, u32[]{:S(2)}, u32[]{:S(2)}) collective-permute-start(f32[1,384,384]{2,1,0:T(8,128)S(1)} %fusion.42), channel_id=1, source_target_pairs={{0,2},{1,3},{2,0},{3,1},{4,6},{5,7},{6,4},{7,5},{8,10},{9,11},{10,... | collective-permute-start | bytes 1769480 | tf_op jit(solution)/shard_map/ppermute | solution.py:68
Sparse Core Ops, SparseCore 0:
  26.6 30.0 all-gather.3
  377.7 30.1 all-gather.5
  699.5 30.8 all-gather.7
